TPU v7x, 32 devices: a whole 2x2x4 slice. The times are simulated.
32 devices in a mesh: seq: 16 (over z, x, core), grp: 2 (over y).
Axes of the slice: x: 2, y: 2, z: 4, core: 2. Of those that a mesh axis runs over, the one named last changes fastest.
Arguments:
- prefill_queries: bfloat16 [1024, 4096], P('seq', 'grp'), may hold values from -6 to 6
- prefill_keys: bfloat16 [1024, 512], P('seq', 'grp'), may hold values from -6 to 6
- prefill_values: bfloat16 [1024, 512], P('seq', 'grp'), may hold values from -6 to 6
- block_mask: int32 [16, 16], replicated, may hold values 0 or 1
- bit_widths: int32 [4], P('grp'), may hold values from 3 to 8
- scale_exps: int32 [4], P('grp'), may hold values from 1 to 4
- decode_queries: bfloat16 [4, 32, 4096], P(None, 'seq', 'grp'), may hold values from -6 to 6
- new_keys: bfloat16 [4, 32, 512], P(None, 'seq', 'grp'), may hold values from -6 to 6
- new_values: bfloat16 [4, 32, 512], P(None, 'seq', 'grp'), may hold values from -6 to 6
- context_len: int32 [32], P('seq'), may hold values from 1 to 1024
Outputs:
- prefill_out: bfloat16 [1024, 4096], P('seq', 'grp')
- decode_out: bfloat16 [4, 32, 4096], P(None, 'seq', 'grp')
All inputs are finite; a program needn't handle non-finite values.
Results may differ from a plain program's by a relative error of at most 0.012.
Values may be sent and summed in bfloat16 or wider, within the bound.
No kernel may reach another device: no remote copies, remote signals or barrier semaphores. Data moves between devices by JAX's collectives and lax.ppermute only.
A program may use at most 64 MiB of HBM per device.

v0:
```python
import math
import jax
import jax.numpy as jnp
from jax import lax
from jax.sharding import PartitionSpec as P

HEADS = 32
KV_HEADS = 4
HEAD = 128
STEPS = 4
very_low = -1e30
norm_eps = 1e-06


def sign_table(order):
    positions = jnp.arange(order, dtype=jnp.int32)
    common_bits = positions[:, None] & positions[None, :]
    parity = jnp.zeros((order, order), jnp.int32)
    for bit_number in range(order.bit_length() - 1):
        parity = parity + (common_bits >> bit_number & 1)
    return (1 - 2 * (parity % 2)).astype(jnp.float32)


def level_terms(bit_widths, scale_exps):
    clip_level = 2.0 ** (bit_widths.astype(jnp.float32) - 1.0) - 1.0
    forward = 2.0 ** scale_exps.astype(jnp.float32) / math.sqrt(HEAD)
    backward = 2.0 ** (-scale_exps.astype(jnp.float32)) / math.sqrt(HEAD)
    return (clip_level, forward, backward)


def online_update(carried, scores, allowed, values, pattern):
    running_max, weight_sum, weighted = carried
    masked = jnp.where(allowed, scores, very_low)
    new_max = jnp.maximum(running_max, jnp.max(masked, axis=-1))
    factor = jnp.exp(running_max - new_max)
    weights = jnp.where(allowed, jnp.exp(masked - new_max[..., None]), 0.0)
    weight_sum = weight_sum * factor + jnp.sum(weights, axis=-1)
    weighted = weighted * factor[..., None] + jnp.einsum(
        pattern, weights.astype(jnp.bfloat16), values, preferred_element_type=jnp.float32
    )
    return (new_max, weight_sum, weighted)


def in_blocks(fold_fn, carried, arrays, offset):
    count_rows = arrays[0].shape[0]
    block_rows = math.gcd(count_rows, 1024)
    if block_rows == count_rows or block_rows < 128:
        return fold_fn(carried, arrays, offset)
    number = count_rows // block_rows
    stacked = tuple((array.reshape((number, block_rows) + array.shape[1:]) for array in arrays))

    def advance(running, scan_item):
        position, pieces = scan_item
        return (fold_fn(running, pieces, offset + position * block_rows), None)

    carried, _ = lax.scan(advance, carried, (jnp.arange(number, dtype=jnp.int32), stacked))
    return carried


def local(
    prefill_queries,
    prefill_keys,
    prefill_values,
    block_mask,
    bit_widths,
    scale_exps,
    decode_queries,
    new_keys,
    new_values,
    context_len,
):
    local_tokens = prefill_queries.shape[0]
    kv_local = bit_widths.shape[0]
    group_size = HEADS // KV_HEADS
    row_count = context_len.shape[0]
    full_width = HEADS * HEAD
    score_scale = 1.0 / math.sqrt(HEAD)
    seq_index = lax.axis_index("seq")
    sign_matrix = sign_table(HEAD).astype(jnp.bfloat16)
    clip_level, forward, backward = level_terms(bit_widths, scale_exps)
    queries = prefill_queries.reshape(local_tokens, kv_local, group_size, HEAD)
    query_pos = seq_index * local_tokens + jnp.arange(local_tokens, dtype=jnp.int32)
    mask_row = block_mask[seq_index]
    block_ids = jnp.arange(mask_row.shape[0], dtype=jnp.int32)

    def encode(rows):
        shaped = rows.reshape(rows.shape[0], kv_local, HEAD)
        rotated = jnp.dot(shaped, sign_matrix, preferred_element_type=jnp.float32)
        levels = jnp.floor(rotated * forward[:, None] + 0.5)
        limited = jnp.clip(levels, -clip_level[:, None], clip_level[:, None])
        return limited.astype(jnp.bfloat16).reshape(rows.shape[0], kv_local * HEAD)

    def restore(rows):
        shaped = rows.reshape(rows.shape[0], kv_local, HEAD)
        restored = jnp.dot(shaped, sign_matrix, preferred_element_type=jnp.float32)
        return (restored * backward[:, None]).astype(jnp.bfloat16)

    def attend(carried, pieces, offset):
        key_rows, value_rows = pieces
        count_rows = key_rows.shape[0]
        key_shaped = key_rows.reshape(count_rows, kv_local, HEAD)
        value_shaped = value_rows.reshape(count_rows, kv_local, HEAD)
        scores = (
            jnp.einsum("tkgd,skd->tkgs", queries, key_shaped, preferred_element_type=jnp.float32)
            * score_scale
        )
        key_pos = offset + jnp.arange(count_rows, dtype=jnp.int32)
        key_block = key_pos // local_tokens
        block_open = jnp.sum(
            jnp.where(key_block[:, None] == block_ids[None, :], mask_row[None, :], 0), axis=1
        )
        allowed = (key_pos[None, :] <= query_pos[:, None]) & (
            (key_block == seq_index) | (block_open == 1)
        )[None, :]
        return online_update(
            carried, scores, allowed[:, None, None, :], value_shaped, "tkgs,skd->tkgd"
        )

    def attend_keep(carried, pieces, offset):
        running, key_store, value_store = carried
        running = in_blocks(attend, running, pieces, offset)
        key_store = encode(pieces[0])
        value_store = encode(pieces[1])
        return (running, key_store, value_store)

    start_shape = (local_tokens, kv_local, group_size)
    start_state = (
        jnp.full(start_shape, very_low, jnp.float32),
        jnp.zeros(start_shape, jnp.float32),
        jnp.zeros(start_shape + (HEAD,), jnp.float32),
    )
    empty_store = jnp.zeros((local_tokens * lax.axis_size("seq"), kv_local * HEAD), jnp.bfloat16)
    fold_fn, initial = (attend_keep, (start_state, empty_store, empty_store))
    folded = fold_fn(
        initial,
        (
            lax.all_gather(prefill_keys, "seq", axis=0, tiled=True),
            lax.all_gather(prefill_values, "seq", axis=0, tiled=True),
        ),
        jnp.int32(0),
    )
    dec_shaped = decode_queries.reshape(STEPS, row_count, kv_local, group_size, HEAD)

    def decode_step(carried, pieces, offset):
        key_rows, value_rows = pieces
        count_rows = key_rows.shape[0]
        key_plain = restore(key_rows)
        value_plain = restore(value_rows)
        scores = (
            jnp.einsum(
                "trkgd,pkd->trkgp", dec_shaped, key_plain, preferred_element_type=jnp.float32
            )
            * score_scale
        )
        key_pos = offset + jnp.arange(count_rows, dtype=jnp.int32)
        allowed = (key_pos[None, :] < context_len[:, None])[None, :, None, None, :]
        return online_update(carried, scores, allowed, value_plain, "trkgp,pkd->trkgd")

    dec_shape = (STEPS, row_count, kv_local, group_size)
    dec_state = (
        jnp.full(dec_shape, very_low, jnp.float32),
        jnp.zeros(dec_shape, jnp.float32),
        jnp.zeros(dec_shape + (HEAD,), jnp.float32),
    )
    prefill_state, key_store, value_store = folded
    dec_state = in_blocks(decode_step, dec_state, (key_store, value_store), jnp.int32(0))
    own_keys = new_keys.reshape(STEPS, row_count, kv_local, HEAD)
    own_values = new_values.reshape(STEPS, row_count, kv_local, HEAD)
    own_scores = (
        jnp.einsum("trkgd,urkd->trkgu", dec_shaped, own_keys, preferred_element_type=jnp.float32)
        * score_scale
    )
    step_pos = jnp.arange(STEPS, dtype=jnp.int32)
    own_open = (step_pos[None, :] <= step_pos[:, None])[:, None, None, None, :]
    dec_state = online_update(dec_state, own_scores, own_open, own_values, "trkgu,urkd->trkgd")
    prefill_attn = (prefill_state[2] / prefill_state[1][..., None]).reshape(
        local_tokens, kv_local * group_size * HEAD
    )
    decode_attn = (dec_state[2] / dec_state[1][..., None]).reshape(
        STEPS, row_count, kv_local * group_size * HEAD
    )
    prefill_squares, decode_squares = lax.psum(
        (
            jnp.sum(prefill_attn * prefill_attn, axis=-1),
            jnp.sum(decode_attn * decode_attn, axis=-1),
        ),
        "grp",
    )
    prefill_out = (
        prefill_attn * lax.rsqrt(prefill_squares[:, None] / full_width + norm_eps)
    ).astype(jnp.bfloat16)
    decode_out = (
        decode_attn * lax.rsqrt(decode_squares[..., None] / full_width + norm_eps)
    ).astype(jnp.bfloat16)
    return (prefill_out, decode_out)


def solution(mesh):
    placed = (
        P("seq", "grp"),
        P("seq", "grp"),
        P("seq", "grp"),
        P(),
        P("grp"),
        P("grp"),
        P(None, "seq", "grp"),
        P(None, "seq", "grp"),
        P(None, "seq", "grp"),
        P("seq"),
    )
    return jax.shard_map(
        local,
        mesh=mesh,
        in_specs=placed,
        out_specs=(P("seq", "grp"), P(None, "seq", "grp")),
        check_vma=False,
    )
```

profile of v0, /device:TPU:0, one launch (start us, length us, event | category | flops | bytes accessed | tf_op | source)
XLA Modules:
  0.0 64.8 jit_solution(13546898876530163890)
XLA Ops:
  0.7 0.7 %copy-done = s32[16,16]{1,0:T(8,128)S(1)} copy-done((s32[16,16]{1,0:T(8,128)S(1)}, s32[16,16]{1,0:T(8,128)}, u32[]{:S(2)}) %copy-start) | copy-done | bytes 1048
  1.3 0.7 %fusion.125 = (bf16[2]{0:T(256)(128)(2,1)S(1)}, bf16[2]{0:T(256)(128)(2,1)S(1)}) fusion(s32[2]{0:T(128)} %param.14), kind=kLoop, calls=%fused_computation.135 | loop fusion | flops 14 | bytes 16 | tf_op jit(solution)/shard_map/neg | solution.py:90
  2.0 0.7 %power_multiply_fusion.1 = (f32[2]{0:T(128)S(1)}, f32[2]{0:T(128)S(1)}) fusion(s32[2]{0:T(128)} %param.15), kind=kLoop, calls=%fused_computation.110 | loop fusion | flops 8 | bytes 24 | tf_op jit(solution)/shard_map/div | solution.py:26
  2.7 0.7 %iota_compare_fusion.2 = pred[2,1024]{1,0:T(4,128)(4,1)S(1)} fusion(s32[2]{0:T(128)} %param.19), kind=kLoop, calls=%fused_computation.94 | loop fusion | flops 2048 | bytes 2056 | tf_op jit(solution)/shard_map/lt | solution.py:156
  3.4 0.7 %reshape.186 = bf16[4,2,2,128]{3,2,1,0:T(2,128)(2,1)S(1)} reshape(bf16[4,2,256]{2,1,0:T(2,128)(2,1)} %param.17) | data formatting | bytes 8192 | tf_op jit(solution)/shard_map/reshape | solution.py:167
  4.1 0.7 %reshape.187 = bf16[4,2,2,128]{3,2,1,0:T(2,128)(2,1)S(1)} reshape(bf16[4,2,256]{2,1,0:T(2,128)(2,1)} %param.18) | data formatting | bytes 8192 | tf_op jit(solution)/shard_map/reshape | solution.py:168
  4.9 0.8 %reshape.185 = bf16[4,2,2,8,128]{4,3,2,1,0:T(8,128)(2,1)S(1)} reshape(bf16[4,2,2048]{2,1,0:T(2,128)(2,1)} %param.16) | data formatting | bytes 65536 | tf_op jit(solution)/shard_map/reshape | solution.py:142
  5.7 0.3 fusion.128
  6.1 1.0 %copy.148 = bf16[8,8,16,128]{3,2,1,0:T(8,128)(2,1)S(1)} copy(bf16[8,8,16,128]{3,1,2,0:T(8,128)(2,1)} %bitcast.106) | data formatting | bytes 524288
  7.1 24.8 %all_gather.6 = bf16[1024,256]{1,0:T(8,128)(2,1)S(1)} all-gather(bf16[64,256]{1,0:T(8,128)(2,1)} %param.11), channel_id=1, replica_groups=mesh['seq'=16,'grp'=2] {'seq'}, dimensions={0}, use_global_device_ids=true | all-gather | bytes 557056 | tf_op jit(solution)/shard_map/all_gather | solution.py:137
  32.1 0.7 %fusion.19 = bf16[1024,2,128,1,1]{2,0,4,3,1:T(8,128)(2,1)S(1)} fusion(bf16[1024,2,128]{0,2,1:T(8,128)(2,1)S(1)} %bitcast.100, bf16[2]{0:T(256)(128)(2,1)S(1)} %get-tuple-element.14, f32[2]{0:T(128)S(1)} %get-tuple-element.16, f32[2]{0:T(128)S(1)} %get-tuple-element.15, bf16[2]{0:T(256)(128)(2,1)S(1)} %get-tuple-element.13), kind=kOutput, calls=%fused_computation.24 | convolution fusion | flops 138018816 | bytes 1048600 | tf_op jit(solution)/shard_map/dot_general | solution.py:95
  32.9 0.4 fusion.129
  33.4 0.2 fusion.48
  33.7 18.9 %all_gather.7 = bf16[1024,256]{1,0:T(8,128)(2,1)S(1)} all-gather(bf16[64,256]{1,0:T(8,128)(2,1)S(1)} %copy-done.1), channel_id=1, replica_groups=mesh['seq'=16,'grp'=2] {'seq'}, dimensions={0}, use_global_device_ids=true | all-gather | bytes 557056 | tf_op jit(solution)/shard_map/all_gather | solution.py:138
  52.8 0.7 %fusion.18 = bf16[1024,2,128,1,1]{2,0,4,3,1:T(8,128)(2,1)S(1)} fusion(bf16[1024,2,128]{0,2,1:T(8,128)(2,1)S(1)} %bitcast.104, bf16[2]{0:T(256)(128)(2,1)S(1)} %get-tuple-element.14, f32[2]{0:T(128)S(1)} %get-tuple-element.16, f32[2]{0:T(128)S(1)} %get-tuple-element.15, bf16[2]{0:T(256)(128)(2,1)S(1)} %get-tuple-element.13), kind=kOutput, calls=%fused_computation.23 | convolution fusion | flops 138018816 | bytes 1048600 | tf_op jit(solution)/shard_map/dot_general | solution.py:95
  53.5 0.3 fusion.33
  53.8 0.3 multiply_reduce_fusion.1
  54.2 0.9 %fusion = (f32[64,2,8]{0,2,1:T(8,128)S(1)}, f32[2,1024,64,8]{1,2,3,0:T(8,128)S(1)}) fusion(pred[64,1024]{1,0:T(8,128)(4,1)S(1)} %fusion.55, bf16[1024,2,128,1]{0,2,3,1:T(8,128)(2,1)S(1)} %bitcast.101, bf16[64,2,8,128]{3,2,1,0:T(8,128)(2,1)S(1)} %bitcast.103), kind=kOutput, calls=%fused_computation.2 | convolution fusion | flops 271580160 | bytes 5050368 | tf_op jit(solution)/shard_map/tkgd,skd->tkgs/dot_general | solution.py:104
  55.1 1.3 %fusion.1 = f32[64,2,8]{0,2,1:T(8,128)S(1)} fusion(f32[2,1024,64,8]{1,2,3,0:T(8,128)S(1)} %get-tuple-element.18, f32[64,2,8]{0,2,1:T(8,128)S(1)} %broadcast_maximum_fusion, pred[64,1024]{1,0:T(8,128)(4,1)S(1)} %fusion.55), kind=kLoop, calls=%fused_computation.3 | loop fusion | flops 5241856 | bytes 4268032 | tf_op jit(solution)/shard_map/reduce_sum | solution.py:37
  56.5 1.4 %multiply_reduce_fusion = (f32[64]{0:T(128)S(1)}, f32[64,2,8,128]{3,0,2,1:T(8,128)S(1)}) fusion(f32[64,2,8]{0,2,1:T(8,128)S(1)} %get-tuple-element.12, bf16[1024,2,128,1]{0,2,3,1:T(8,128)(2,1)S(1)} %bitcast.105, f32[2,1024,64,8]{1,2,3,0:T(8,128)S(1)} %get-tuple-element.18, f32[64,2,8]{0,2,1:T(8,128)S(1)} %broadcast_maximum_fusion, ...), kind=kOutput, calls=%fused_computation.53 | convolution fusion | flops 274202560 | bytes 5320960 | tf_op jit(solution)/shard_map/tkgs,skd->tkgd/dot_general | solution.py:38
  57.9 4.9 %all-reduce = (f32[64]{0:T(128)S(1)}, f32[4,2]{1,0:T(4,128)S(1)}) all-reduce(f32[64]{0:T(128)S(1)} %get-tuple-element.19, f32[4,2]{1,0:T(4,128)S(1)} %get-tuple-element.25), channel_id=1, replica_groups=mesh['seq'=16,'grp'=2] {'grp'}, use_global_device_ids=true, to_apply=%region_4.5 | all-reduce | flops 72 | bytes 576 | tf_op jit(solution)/shard_map/psum | solution.py:182
  62.8 0.7 %multiply_convert_fusion = bf16[4,2,2048]{2,1,0:T(2,128)(2,1)} fusion(f32[4,2,2048]{2,1,0:T(2,128)S(1)} %reshape.188, f32[4,2]{1,0:T(4,128)S(1)} %add_rsqrt_fusion), kind=kLoop, calls=%fused_computation.71 | loop fusion | flops 32768 | bytes 98336 | tf_op jit(solution)/shard_map/convert_element_type | solution.py:194
  63.6 0.3 copy.107
  63.9 0.9 %fusion.39 = bf16[64,2048]{1,0:T(8,128)(2,1)} fusion(f32[8,8,16,128]{3,2,1,0:T(8,128)S(1)} %bitcast.102, f32[64]{0:T(128)S(1)} %add_rsqrt_fusion.1), kind=kLoop, calls=%fused_computation.43 | loop fusion | flops 262144 | bytes 786688 | tf_op jit(solution)/shard_map/convert_element_type | solution.py:191
  (25 shorter events, 0.9 us)
Async XLA Ops:
  0.6 0.7 %copy-start = (s32[16,16]{1,0:T(8,128)S(1)}, s32[16,16]{1,0:T(8,128)}, u32[]{:S(2)}) copy-start(s32[16,16]{1,0:T(8,128)} %param.13) | copy-start | bytes 3076
  0.6 33.1 %copy-start.1 = (bf16[64,256]{1,0:T(8,128)(2,1)S(1)}, bf16[64,256]{1,0:T(8,128)(2,1)}, u32[]{:S(2)}) copy-start(bf16[64,256]{1,0:T(8,128)(2,1)} %param.12) | copy-start | bytes 98308
where the time goes:
time: 65.2 us; the launch traced here: 64.8 us
  blocking collectives  48.6 us (75%)
  other arithmetic  5.65 us (9%)
  matrix products  5.04 us (8%)
  local copies, waits for them, and re-layouts  4.63 us (7%)
  between operations  0.81 us (1%)
    all_gather x1, blocking collectives, local(): lax.all_gather(prefill_keys, 'seq', axis=0, tiled=True)  24.8 us
    all_gather x1, blocking collectives, local(): lax.all_gather(prefill_values, 'seq', axis=0, tiled=True)  18.9 us
    psum x1, blocking collectives, local(): lax.psum((jnp.sum(prefill_attn * prefill_attn, axis=-1), jnp.sum(decode_a...  4.93 us
    dot_general x3, matrix products, online_update(): jnp.einsum(pattern, weights.astype(jnp.bfloat16), values, preferred_eleme...  2.03 us
    unnamed x5, local copies, waits for them, and re-layouts  1.66 us
    reduce_sum x2, other arithmetic, online_update(): weight_sum = weight_sum * factor + jnp.sum(weights, axis=-1)  1.6 us
    dot_general x2, matrix products, restore(): restored = jnp.dot(shaped, sign_matrix, preferred_element_type=jnp.float32)  1.46 us

commit v1 on v0

--- a/solution.py
+++ b/solution.py
@@ -1,3 +1,4 @@
+import functools
 import math
 import jax
 import jax.numpy as jnp
@@ -10,6 +11,18 @@
 STEPS = 4
 very_low = -1e30
 norm_eps = 1e-06
+
+
+def pack_paths_up(local_block, peer_axis):
+    leaves = []
+    for _ in range(jax.lax.axis_size(peer_axis)):
+        leaves.append(local_block)
+    mixed_arr = jnp.stack(leaves, 0)
+    local_out = jax.lax.all_to_all(mixed_arr, peer_axis, 0, 0)
+    return jnp.concatenate(local_out, axis=0)
+
+
+search_bands = functools.partial(pack_paths_up, peer_axis="seq")
 
 
 def sign_table(order):
@@ -133,10 +146,7 @@
     fold_fn, initial = (attend_keep, (start_state, empty_store, empty_store))
     folded = fold_fn(
         initial,
-        (
-            lax.all_gather(prefill_keys, "seq", axis=0, tiled=True),
-            lax.all_gather(prefill_values, "seq", axis=0, tiled=True),
-        ),
+        (search_bands(prefill_keys), lax.all_gather(prefill_values, "seq", axis=0, tiled=True)),
         jnp.int32(0),
     )
     dec_shaped = decode_queries.reshape(STEPS, row_count, kv_local, group_size, HEAD)

time: 65.2 us -> 52.8 us (0.81)
  blocking collectives: 48.6 us -> 28.4 us
  starting transfers between devices: 0 us -> 7.39 us
  local copies, waits for them, and re-layouts: 4.63 us -> 5.51 us
  other arithmetic: 5.65 us -> 4.98 us
    all_gather x1 -> x0, blocking collectives: 24.8 us -> none  [local(): lax.all_gather(prefill_keys, 'seq', axis=0, tiled=True)]
    all_to_all x0 -> x1, starting transfers between devices: none -> 7.39 us  [pack_paths_up(): local_out = jax.lax.all_to_all(mixed_arr, peer_axis, 0, 0)]
    all_gather x1, blocking collectives: 18.9 us -> 23.5 us  [local(): lax.all_gather(prefill_values, 'seq', axis=0, tiled=True)]
    another operation x0 -> x2, local copies, waits for them, and re-layouts: none -> 1.73 us  [the longest x1 1.61 us: pack_paths_up(): mixed_arr = jnp.stack(leaves, 0)]
    unnamed x5, local copies, waits for them, and re-layouts: 1.66 us -> 1 us
    lt x1, other arithmetic: 0.73 us -> 0.08 us  [decode_step(): allowed = (key_pos[None, :] < context_len[:, None])[None, :, None, None, :]]
  transfers between devices with their start and end apart: 0 -> 1, of which waited for: 0 -> 0; matrix products, arithmetic and copies ran while one was open for 0% -> 11% of each run, Pallas kernels for 0% -> 0%
where the time goes in v1:
time: 52.8 us; the launch traced here: 52.3 us
  blocking collectives  28.4 us (54%)
  starting transfers between devices  7.39 us (14%)
  local copies, waits for them, and re-layouts  5.51 us (10%)
  matrix products  5.09 us (10%)
  other arithmetic  4.98 us (9%)
  between operations  0.85 us (2%)
    all_gather x1, blocking collectives, local(): lax.all_gather(prefill_values, 'seq', axis=0, tiled=True)  23.5 us
    all_to_all x1, starting transfers between devices, pack_paths_up(): local_out = jax.lax.all_to_all(mixed_arr, peer_axis, 0, 0)  7.39 us
    psum x1, blocking collectives, local(): lax.psum((jnp.sum(prefill_attn * prefill_attn, axis=-1), jnp.sum(decode_a...  4.93 us
    dot_general x3, matrix products, online_update(): jnp.einsum(pattern, weights.astype(jnp.bfloat16), values, preferred_eleme...  2.03 us
    another operation x1, local copies, waits for them, and re-layouts, pack_paths_up(): mixed_arr = jnp.stack(leaves, 0)  1.61 us
    reduce_sum x2, other arithmetic, online_update(): weight_sum = weight_sum * factor + jnp.sum(weights, axis=-1)  1.59 us
    dot_general x2, matrix products, restore(): restored = jnp.dot(shaped, sign_matrix, preferred_element_type=jnp.float32)  1.45 us
  transfers between devices with their start and end apart: 1, of which 0 were waited for; matrix products, arithmetic and copies ran while one was open for 11% of the time, Pallas kernels for 0%

profile of v1, /device:TPU:0, one launch (start us, length us, event | category | flops | bytes accessed | tf_op | source)
XLA Modules:
  0.0 52.3 jit_solution(15541897155891013883)
XLA Ops:
  0.7 1.6 %stack.2 = bf16[16,64,256]{2,1,0:T(8,128)(2,1)} broadcast(bf16[64,256]{1,0:T(8,128)(2,1)} %param.11), dimensions={1,2} | broadcast | bytes 557056 | tf_op jit(solution)/shard_map/stack | solution.py:20
  2.3 7.4 %all-to-all-start = ((bf16[16,64,256]{2,1,0:T(8,128)(2,1)}), bf16[16,64,256]{2,1,0:T(8,128)(2,1)S(1)}, u32[]{:S(2)}, u32[]{:S(2)}) async-start(bf16[16,64,256]{2,1,0:T(8,128)(2,1)} %stack.2), calls=%async_computation | async-start | bytes 1048576 | tf_op jit(solution)/shard_map/all_to_all | solution.py:21
  9.7 0.7 %fusion.128 = (bf16[2]{0:T(256)(128)(2,1)S(1)}, bf16[2]{0:T(256)(128)(2,1)S(1)}) fusion(s32[2]{0:T(128)} %param.14), kind=kLoop, calls=%fused_computation.137 | loop fusion | flops 14 | bytes 16 | tf_op jit(solution)/shard_map/neg | solution.py:103
  10.4 0.7 %power_multiply_fusion.1 = (f32[2]{0:T(128)S(1)}, f32[2]{0:T(128)S(1)}) fusion(s32[2]{0:T(128)} %param.15), kind=kLoop, calls=%fused_computation.112 | loop fusion | flops 8 | bytes 24 | tf_op jit(solution)/shard_map/div | solution.py:39
  11.0 0.7 %reshape.183 = bf16[4,2,2,128]{3,2,1,0:T(2,128)(2,1)S(1)} reshape(bf16[4,2,256]{2,1,0:T(2,128)(2,1)} %param.17) | data formatting | bytes 8192 | tf_op jit(solution)/shard_map/reshape | solution.py:177
  11.7 0.7 %reshape.184 = bf16[4,2,2,128]{3,2,1,0:T(2,128)(2,1)S(1)} reshape(bf16[4,2,256]{2,1,0:T(2,128)(2,1)} %param.18) | data formatting | bytes 8192 | tf_op jit(solution)/shard_map/reshape | solution.py:178
  12.4 0.8 %reshape.182 = bf16[4,2,2,8,128]{4,3,2,1,0:T(8,128)(2,1)S(1)} reshape(bf16[4,2,2048]{2,1,0:T(2,128)(2,1)} %param.16) | data formatting | bytes 65536 | tf_op jit(solution)/shard_map/reshape | solution.py:152
  13.2 1.0 %copy.142 = bf16[8,8,16,128]{3,2,1,0:T(8,128)(2,1)S(1)} copy(bf16[8,8,16,128]{3,1,2,0:T(8,128)(2,1)} %bitcast.99) | data formatting | bytes 524288
  14.2 23.5 %all_gather.3 = bf16[1024,256]{1,0:T(8,128)(2,1)S(1)} all-gather(bf16[64,256]{1,0:T(8,128)(2,1)} %param.12), channel_id=1, replica_groups=mesh['seq'=16,'grp'=2] {'seq'}, dimensions={0}, use_global_device_ids=true | all-gather | bytes 557056 | tf_op jit(solution)/shard_map/all_gather | solution.py:149
  37.7 0.2 copy.100
  38.0 0.7 %fusion.18 = bf16[1024,2,128,1,1]{2,0,4,3,1:T(8,128)(2,1)S(1)} fusion(bf16[1024,2,128]{0,2,1:T(8,128)(2,1)S(1)} %bitcast.97, bf16[2]{0:T(256)(128)(2,1)S(1)} %get-tuple-element.14, f32[2]{0:T(128)S(1)} %get-tuple-element.16, f32[2]{0:T(128)S(1)} %get-tuple-element.15, bf16[2]{0:T(256)(128)(2,1)S(1)} %get-tuple-element.13), kind=kOutput, calls=%fused_computation.23 | convolution fusion | flops 138018816 | bytes 1048600 | tf_op jit(solution)/shard_map/dot_general | solution.py:108
  39.0 0.3 fusion.131
  39.4 0.7 %fusion.19 = bf16[1024,2,128,1,1]{2,0,4,3,1:T(8,128)(2,1)S(1)} fusion(bf16[1024,2,128]{2,1,0:T(2,128)(2,1)S(1)} %reshape_reshape.4, bf16[2]{0:T(256)(128)(2,1)S(1)} %get-tuple-element.14, f32[2]{0:T(128)S(1)} %get-tuple-element.16, f32[2]{0:T(128)S(1)} %get-tuple-element.15, bf16[2]{0:T(256)(128)(2,1)S(1)} %get-tuple-element.13), kind=kOutput, calls=%fused_computation.24 | convolution fusion | flops 138018816 | bytes 1048600 | tf_op jit(solution)/shard_map/dot_general | solution.py:108
  40.2 0.4 fusion.132
  40.7 0.2 fusion.52
  41.0 0.3 fusion.33
  41.3 0.3 multiply_reduce_fusion.1
  41.6 0.9 %fusion = (f32[64,2,8]{0,2,1:T(8,128)S(1)}, f32[2,1024,64,8]{1,2,3,0:T(8,128)S(1)}) fusion(pred[64,1024]{1,0:T(8,128)(4,1)S(1)} %fusion.58, bf16[64,2,8,128]{3,2,1,0:T(8,128)(2,1)S(1)} %bitcast.96, bf16[1024,2,128,1]{2,1,0,3:T(2,128)(2,1)S(1)} %bitcast.94), kind=kOutput, calls=%fused_computation.2 | convolution fusion | flops 271580160 | bytes 5050368 | tf_op jit(solution)/shard_map/tkgd,skd->tkgs/dot_general | solution.py:117
  42.6 1.3 %fusion.1 = f32[64,2,8]{0,2,1:T(8,128)S(1)} fusion(f32[2,1024,64,8]{1,2,3,0:T(8,128)S(1)} %get-tuple-element.18, f32[64,2,8]{0,2,1:T(8,128)S(1)} %broadcast_maximum_fusion, pred[64,1024]{1,0:T(8,128)(4,1)S(1)} %fusion.58), kind=kLoop, calls=%fused_computation.3 | loop fusion | flops 5241856 | bytes 4268032 | tf_op jit(solution)/shard_map/reduce_sum | solution.py:50
  44.0 1.4 %multiply_reduce_fusion = (f32[64]{0:T(128)S(1)}, f32[64,2,8,128]{3,0,2,1:T(8,128)S(1)}) fusion(f32[64,2,8]{0,2,1:T(8,128)S(1)} %get-tuple-element.12, bf16[1024,2,128,1]{0,2,3,1:T(8,128)(2,1)S(1)} %bitcast.98, f32[2,1024,64,8]{1,2,3,0:T(8,128)S(1)} %get-tuple-element.18, f32[64,2,8]{0,2,1:T(8,128)S(1)} %broadcast_maximum_fusion, ...), kind=kOutput, calls=%fused_computation.56 | convolution fusion | flops 274202560 | bytes 5320960 | tf_op jit(solution)/shard_map/tkgs,skd->tkgd/dot_general | solution.py:51
  45.4 4.9 %all-reduce = (f32[64]{0:T(128)S(1)}, f32[4,2]{1,0:T(4,128)S(1)}) all-reduce(f32[64]{0:T(128)S(1)} %get-tuple-element.19, f32[4,2]{1,0:T(4,128)S(1)} %get-tuple-element.25), channel_id=1, replica_groups=mesh['seq'=16,'grp'=2] {'grp'}, use_global_device_ids=true, to_apply=%region_4.5 | all-reduce | flops 72 | bytes 576 | tf_op jit(solution)/shard_map/psum | solution.py:192
  50.3 0.3 copy.102
  50.7 0.7 %multiply_convert_fusion = bf16[4,2,2048]{2,1,0:T(2,128)(2,1)} fusion(f32[4,2,2048]{2,1,0:T(2,128)S(1)} %reshape.185, f32[4,2]{1,0:T(4,128)S(1)} %add_rsqrt_fusion), kind=kLoop, calls=%fused_computation.73 | loop fusion | flops 32768 | bytes 98336 | tf_op jit(solution)/shard_map/convert_element_type | solution.py:204
  51.4 0.9 %fusion.39 = bf16[64,2048]{1,0:T(8,128)(2,1)} fusion(f32[8,8,16,128]{3,2,1,0:T(8,128)S(1)} %bitcast.95, f32[64]{0:T(128)S(1)} %add_rsqrt_fusion.1), kind=kLoop, calls=%fused_computation.43 | loop fusion | flops 262144 | bytes 786688 | tf_op jit(solution)/shard_map/convert_element_type | solution.py:201
  (27 shorter events, 0.7 us)
Async XLA Ops:
  0.6 37.3 %copy-start = (s32[16,16]{1,0:T(8,128)S(1)}, s32[16,16]{1,0:T(8,128)}, u32[]{:S(2)}) copy-start(s32[16,16]{1,0:T(8,128)} %param.13) | copy-start | bytes 3076
  0.6 38.1 %copy-start.1 = (s32[2]{0:T(128)S(1)}, s32[2]{0:T(128)}, u32[]{:S(2)}) copy-start(s32[2]{0:T(128)} %param.19) | copy-start | bytes 28
  2.3 37.0 %all-to-all-start = ((bf16[16,64,256]{2,1,0:T(8,128)(2,1)}), bf16[16,64,256]{2,1,0:T(8,128)(2,1)S(1)}, u32[]{:S(2)}, u32[]{:S(2)}) async-start(bf16[16,64,256]{2,1,0:T(8,128)(2,1)} %stack.2), calls=%async_computation | async-start | bytes 1048576 | tf_op jit(solution)/shard_map/all_to_all | solution.py:21
